TPU v7x, 512 devices: a whole 4x4x16 slice. The times are simulated.
512 devices in a mesh: tm: 8 (over x, core), pair: 64 (over z, y).
Axes of the slice: x: 4, y: 4, z: 16, core: 2. Of those that a mesh axis runs over, the one named last changes fastest.
Arguments:
- traces: float32 [16, 8192, 1024], P('tm', 'pair'), may hold values from -6 to 6
- owner: int32 [64], replicated, may hold values from 0 to 63, each once
- tiles: int32 [192, 2], P('pair'), may hold values from 0 to 63, as said below
- counts: int32 [64], P('pair'), may hold values from 1 to 3, as said below
Outputs:
- stacks: float32 [192, 128, 16384], P('pair', None, 'tm')
Inputs may be any that keep to these rules, and one draw needn't show every extreme that they name: `tiles`: each row names fiber blocks a <= b with b - a at most 6. `counts`: the first that many of an index's 3 slots are live; some index has all 3 live.
All inputs are finite; a program needn't handle non-finite values.
Results may differ from a plain program's by a relative error of at most 0.0038.
Values may be sent and summed in bfloat16 or wider, within the bound.
A program may use at most 64 MiB of HBM per device.

v0:
```python
import math
import jax
import jax.numpy as jnp
from jax import lax
from jax.sharding import PartitionSpec as P

NT = 1024
NF = 128
LOW_BIN = 8
LAGS = 128


def forward_table():
    samples = jnp.arange(NT, dtype=jnp.int32)
    bins = LOW_BIN + jnp.arange(NF, dtype=jnp.int32)
    phase = samples[:, None] * bins[None, :] % NT
    angle = phase.astype(jnp.float32) * (2.0 * math.pi / NT)
    return jnp.concatenate([jnp.cos(angle), -jnp.sin(angle)], axis=1)


def inverse_table():
    shifts = jnp.arange(LAGS, dtype=jnp.int32) - LAGS // 2
    bins = LOW_BIN + jnp.arange(NF, dtype=jnp.int32)
    phase = jnp.mod(shifts[:, None] * bins[None, :], NT)
    angle = phase.astype(jnp.float32) * (2.0 * math.pi / NT)
    return (jnp.cos(angle), -jnp.sin(angle))


def window_sum(values):
    widths = [(0, 0)] * (values.ndim - 1) + [(2, 2)]
    padded = jnp.pad(values, widths)
    total = padded[..., 0:NF]
    for offset in range(1, 5):
        total = total + padded[..., offset : offset + NF]
    return total


def whiten(spectrum):
    real_part = spectrum[..., :NF]
    imag_part = spectrum[..., NF:]
    power = real_part * real_part + imag_part * imag_part
    counted = window_sum(jnp.ones((NF,), jnp.float32))
    smooth = window_sum(power) / counted
    level = jnp.mean(power, axis=-1, keepdims=True)
    factor = lax.rsqrt(smooth + 0.05 * level + 1e-06)
    return jnp.concatenate([real_part * factor, imag_part * factor], axis=-1).astype(jnp.bfloat16)


def lookup(owner, fiber_ids):
    onehot = fiber_ids[..., None] == jnp.arange(owner.shape[0], dtype=jnp.int32)
    return jnp.sum(jnp.where(onehot, owner, 0), axis=-1)


def shards(traces, owner, tiles, counts):
    seg_count, block, samples = traces.shape
    rows = seg_count * block
    width = 2 * NF
    spectrum = jnp.dot(
        traces.reshape(rows, samples), forward_table(), precision=lax.Precision.HIGHEST
    )
    white = whiten(spectrum)
    time_count = lax.axis_size("tm")
    segments = seg_count * time_count
    share = block // time_count
    slots = tiles.shape[0]
    scale = 1.0 / math.sqrt(segments * NF)
    cos_part, sin_part = inverse_table()
    every = lax.all_gather(white[None], "pair", axis=0, tiled=True)
    stored = lookup(owner, tiles)
    picked = jnp.take(every, stored.reshape(-1), axis=0).reshape(slots, 2, rows, width)
    number = picked.shape[0]
    left = picked[:, 0].reshape(number, seg_count, block, width)
    right = picked[:, 1].reshape(number, seg_count, block, width)
    left_all = lax.all_to_all(left, "tm", split_axis=2, concat_axis=1, tiled=True)
    right_all = lax.all_gather(right, "tm", axis=1, tiled=True)
    left_real = left_all[..., :NF]
    left_imag = left_all[..., NF:]
    right_real = right_all[..., :NF]
    right_imag = right_all[..., NF:]
    cross_real = jnp.einsum(
        "qsif,qsjf->qfij", left_real, right_real, preferred_element_type=jnp.float32
    )
    cross_real = cross_real + jnp.einsum(
        "qsif,qsjf->qfij", left_imag, right_imag, preferred_element_type=jnp.float32
    )
    cross_imag = jnp.einsum(
        "qsif,qsjf->qfij", left_real, right_imag, preferred_element_type=jnp.float32
    )
    cross_imag = cross_imag - jnp.einsum(
        "qsif,qsjf->qfij", left_imag, right_real, preferred_element_type=jnp.float32
    )
    cross_real = cross_real.reshape(number, NF, share * block)
    cross_imag = cross_imag.reshape(number, NF, share * block)
    lagged = jnp.einsum("lf,qfx->qlx", cos_part, cross_real, precision=lax.Precision.HIGHEST)
    lagged = lagged + jnp.einsum(
        "lf,qfx->qlx", sin_part, cross_imag, precision=lax.Precision.HIGHEST
    )
    partial_value = lagged * scale
    live = (jnp.arange(slots, dtype=jnp.int32) < counts[0]).astype(jnp.float32)
    return partial_value * live[:, None, None]


def solution(mesh):
    placed = (P("tm", "pair", None), P(), P("pair", None), P("pair"))
    return jax.shard_map(
        shards, mesh=mesh, in_specs=placed, out_specs=P("pair", None, "tm"), check_vma=False
    )
```

profile of v0, /device:TPU:1, one launch (start us, length us, event | category | flops | bytes accessed | tf_op | source)
XLA Modules:
  0.0 259.8 jit_solution(12651376614939929892)
XLA Ops:
  6.6 2.1 fusion.9
  8.6 1.8 convolution_bitcast_fusion
  10.8 0.8 copy.56
  12.0 154.2 %all-gather.3.cloned.1.call-done = bf16[64,256,256]{2,1,0:T(8,128)(2,1)} async-done(((bf16[1,256,256]{2,1,0:T(8,128)(2,1)}), bf16[64,256,256]{2,1,0:T(8,128)(2,1)}) %all-gather.3.cloned.1.call-update) | async-done | bytes 8388624 | tf_op jit(solution)/shard_map/all_gather | solution.py:68
  166.3 4.0 %gather_fusion = bf16[6,256,256]{2,1,0:T(8,128)(2,1)S(1)} fusion(bf16[64,256,256]{2,1,0:T(8,128)(2,1)} %all-gather.3.cloned.1.call-done, s32[1024]{0:T(1024)S(1)} %pad_clamp_fusion), kind=kCustom, calls=%fused_computation | custom fusion | bytes 1572888 | tf_op jit(solution)/shard_map/jit(_take)/gather | solution.py:70
  170.5 0.8 copy.61
  171.3 1.2 copy.57
  172.4 12.6 %all-to-all-start = ((bf16[3,2,128,256]{3,1,0,2:T(2,128)(2,1)}), bf16[3,2,128,256]{3,1,0,2:T(2,128)(2,1)S(1)}, u32[]{:S(2)}, u32[]{:S(2)}) async-start(bf16[3,2,128,256]{3,1,0,2:T(2,128)(2,1)} %copy.57), calls=%async_computation | async-start | bytes 786432 | tf_op jit(solution)/shard_map/all_to_all | solution.py:74
  185.6 7.4 %all-to-all-done = bf16[3,2,128,256]{3,1,0,2:T(2,128)(2,1)S(1)} async-done(((bf16[3,2,128,256]{3,1,0,2:T(2,128)(2,1)}), bf16[3,2,128,256]{3,1,0,2:T(2,128)(2,1)S(1)}, u32[]{:S(2)}, u32[]{:S(2)}) %all-to-all-start) | async-done | bytes 393248 | tf_op jit(solution)/shard_map/all_to_all | solution.py:74
  193.2 1.7 copy.72
  194.9 1.1 copy.74
  196.0 13.7 %all-gather.5.cloned.1.call-done = bf16[3,16,128,256]{3,2,0,1:T(8,128)(2,1)} async-done(((bf16[3,2,128,256]{3,2,0,1:T(8,128)(2,1)}), bf16[3,16,128,256]{3,2,0,1:T(8,128)(2,1)}) %all-gather.5.cloned.1.call-update) | async-done | bytes 3145744 | tf_op jit(solution)/shard_map/all_gather | solution.py:75
  209.8 4.0 %fusion.39 = (bf16[3,16,128,128]{3,2,0,1:T(8,128)(2,1)}, bf16[3,16,128,128]{3,2,0,1:T(8,128)(2,1)}) fusion(bf16[3,16,128,256]{3,2,0,1:T(8,128)(2,1)} %all-gather.5.cloned.1.call-done), kind=kLoop, calls=%fused_computation.71 | loop fusion | bytes 6291456 | tf_op jit(solution)/shard_map/slice | solution.py:79
  213.7 2.8 %copy.75 = bf16[3,16,128,128]{2,1,3,0:T(8,128)(2,1)} copy(bf16[3,16,128,128]{3,2,0,1:T(8,128)(2,1)} %get-tuple-element.9) | data formatting | bytes 3145728
  216.5 2.8 %copy.73 = bf16[3,16,128,128]{2,1,3,0:T(8,128)(2,1)} copy(bf16[3,16,128,128]{3,2,0,1:T(8,128)(2,1)} %get-tuple-element.10) | data formatting | bytes 3145728
  219.3 3.0 %fusion.43 = f32[3,128,16,128]{3,2,1,0:T(8,128)S(1)} fusion(bf16[3,16,16,128]{1,2,3,0:T(8,128)(2,1)} %copy.72, bf16[3,16,128,128]{2,1,3,0:T(8,128)(2,1)} %copy.75), kind=kOutput, calls=%fused_computation.75 | convolution fusion | flops 25165824 | bytes 4915200 | tf_op jit(solution)/shard_map/qsif,qsjf->qfij/dot_general | solution.py:86
  222.3 2.6 %fusion.42 = f32[3,128,16,128]{3,2,1,0:T(8,128)} fusion(bf16[3,16,16,128]{1,2,3,0:T(8,128)(2,1)S(1)} %copy-done.1, bf16[3,16,128,128]{2,1,3,0:T(8,128)(2,1)S(1)} %copy-done.2), kind=kOutput, calls=%fused_computation.74 | convolution fusion | flops 25165824 | bytes 4915200 | tf_op jit(solution)/shard_map/qsif,qsjf->qfij/dot_general | solution.py:80
  225.0 2.6 %convolution_subtract_fusion = f32[3,128,16,128]{3,2,1,0:T(8,128)} fusion(f32[3,128,16,128]{3,2,1,0:T(8,128)S(1)} %fusion.43, bf16[3,16,16,128]{1,2,3,0:T(8,128)(2,1)S(1)} %copy.74, bf16[3,16,128,128]{2,1,3,0:T(8,128)(2,1)S(1)} %copy-done.2), kind=kOutput, calls=%fused_computation.2 | convolution fusion | flops 25952256 | bytes 8060928 | tf_op jit(solution)/shard_map/qsif,qsjf->qfij/dot_general | solution.py:89
  227.6 3.5 %copy.71 = f32[3,128,16,128]{1,3,2,0:T(8,128)} copy(f32[3,128,16,128]{3,2,1,0:T(8,128)} %convolution_subtract_fusion) | data formatting | bytes 6291456 | tf_op jit(solution)/shard_map/reshape | solution.py:93
  231.1 5.0 %convolution_add_fusion = f32[3,128,16,128]{3,2,1,0:T(8,128)} fusion(f32[3,128,16,128]{3,2,1,0:T(8,128)} %fusion.42, bf16[3,16,16,128]{1,2,3,0:T(8,128)(2,1)S(1)} %copy.74, bf16[3,16,128,128]{2,1,3,0:T(8,128)(2,1)} %copy.75), kind=kOutput, calls=%fused_computation.3 | convolution fusion | flops 25952256 | bytes 8060928 | tf_op jit(solution)/shard_map/qsif,qsjf->qfij/dot_general | solution.py:83
  236.1 3.6 %copy.70 = f32[3,128,16,128]{1,3,2,0:T(8,128)} copy(f32[3,128,16,128]{3,2,1,0:T(8,128)} %convolution_add_fusion) | data formatting | bytes 6291456 | tf_op jit(solution)/shard_map/reshape | solution.py:92
  239.7 5.0 %fusion.16 = f32[3,2048,128]{2,1,0:T(8,128)S(1)} fusion(f32[3,128,2048]{1,2,0:T(8,128)} %bitcast.41, s32[128]{0:T(128)S(1)} %get-tuple-element.18, s32[128]{0:T(128)S(1)} %get-tuple-element.17), kind=kOutput, calls=%fused_computation.37 | convolution fusion | flops 1208188928 | bytes 6292480 | tf_op jit(solution)/shard_map/lf,qfx->qlx/dot_general | solution.py:94
  244.7 4.7 %multiply_bitcast_fusion = f32[3,128,2048]{1,2,0:T(8,128)} fusion(f32[3,2048,128]{2,1,0:T(8,128)S(1)} %fusion.16, f32[3,128,2048]{1,2,0:T(8,128)S(1)} %bitcast.40, f32[3]{0:T(128)S(1)} %compare_select_fusion.3, s32[128]{0:T(128)S(1)} %get-tuple-element.18, s32[128]{0:T(128)S(1)} %get-tuple-element.17), kind=kOutput, calls=%fused_computation.1 | convolution fusion | flops 1209778176 | bytes 9438220 | tf_op jit(solution)/shard_map/lf,qfx->qlx/dot_general | solution.py:95
  249.4 3.5 %copy.67 = f32[3,128,2048]{2,1,0:T(8,128)} copy(f32[3,128,2048]{1,2,0:T(8,128)} %multiply_bitcast_fusion) | data formatting | bytes 6291456 | tf_op jit(solution)/shard_map/mul | solution.py:100
  (36 shorter events, 1.1 us)
Async XLA Ops:
  6.5 2.1 copy-start
  6.5 5.1 %copy-start.4 = (s32[3,2]{0,1:T(2,128)S(1)}, s32[3,2]{0,1:T(2,128)}, u32[]{:S(2)}) copy-start(s32[3,2]{0,1:T(2,128)} %param.6) | copy-start | bytes 76
  6.5 5.2 %copy-start.5 = (s32[64]{0:T(128)S(1)}, s32[64]{0:T(128)}, u32[]{:S(2)}) copy-start(s32[64]{0:T(128)} %param.5) | copy-start | bytes 772
  6.5 159.7 %all-gather.3.cloned.1.call-start = ((), (), s32[]{:S(2)}) async-start(), calls=%async_computation.1 | async-start | bytes 8519680 | tf_op jit(solution)/shard_map/all_gather | solution.py:68
  11.6 198.2 %all-gather.5.cloned.1.call-start = ((), (), s32[]{:S(2)}) async-start(), calls=%async_computation.2 | async-start | bytes 3538944 | tf_op jit(solution)/shard_map/all_gather | solution.py:75
  172.4 20.6 %all-to-all-start = ((bf16[3,2,128,256]{3,1,0,2:T(2,128)(2,1)}), bf16[3,2,128,256]{3,1,0,2:T(2,128)(2,1)S(1)}, u32[]{:S(2)}, u32[]{:S(2)}) async-start(bf16[3,2,128,256]{3,1,0,2:T(2,128)(2,1)} %copy.57), calls=%async_computation | async-start | bytes 786432 | tf_op jit(solution)/shard_map/all_to_all | solution.py:74
  219.3 3.0 %copy-start.1 = (bf16[3,16,16,128]{1,2,3,0:T(8,128)(2,1)S(1)}, bf16[3,16,16,128]{1,2,3,0:T(8,128)(2,1)}, u32[]{:S(2)}) copy-start(bf16[3,16,16,128]{1,2,3,0:T(8,128)(2,1)} %copy.72) | copy-start | bytes 589828
  219.3 3.0 %copy-start.2 = (bf16[3,16,128,128]{2,1,3,0:T(8,128)(2,1)S(1)}, bf16[3,16,128,128]{2,1,3,0:T(8,128)(2,1)}, u32[]{:S(2)}) copy-start(bf16[3,16,128,128]{2,1,3,0:T(8,128)(2,1)} %copy.73) | copy-start | bytes 4718596
  239.7 5.0 %copy-start.3 = (f32[3,128,16,128]{1,3,2,0:T(8,128)S(1)}, f32[3,128,16,128]{1,3,2,0:T(8,128)}, u32[]{:S(2)}) copy-start(f32[3,128,16,128]{1,3,2,0:T(8,128)} %copy.71) | copy-start | bytes 9437188
Sparse Core Ops, SparseCore 0:
  11.7 154.5 all-gather.2
  171.4 38.3 all-gather.4
where the time goes:
time: 260 us
  waiting for transfers between devices  175 us (67%)
  local copies, waits for them, and re-layouts  30.1 us (12%)
  matrix products  24.7 us (10%)
  between operations  14.2 us (5%)
  starting transfers between devices  12.6 us (5%)
  other arithmetic  2.73 us (1%)
    all_gather x1, waiting for transfers between devices, shards(): every = lax.all_gather(white[None], 'pair', axis=0, tiled=True)  154 us
    all_gather x1, waiting for transfers between devices, shards(): right_all = lax.all_gather(right, 'tm', axis=1, tiled=True)  13.7 us
    all_to_all x1, starting transfers between devices, shards(): lax.all_to_all(left, 'tm', split_axis=2, concat_axis=1, tiled=True)  12.6 us
    unnamed x17, local copies, waits for them, and re-layouts  8.55 us
    all_to_all x1, waiting for transfers between devices, shards(): lax.all_to_all(left, 'tm', split_axis=2, concat_axis=1, tiled=True)  7.41 us
  transfers between devices with their start and end apart: 3, of which 3 were waited for; matrix products, arithmetic and copies ran while one was open for 2% of the time, Pallas kernels for 0%

commit v1 on v0

--- a/solution.py
+++ b/solution.py
@@ -72,7 +72,9 @@
     left = picked[:, 0].reshape(number, seg_count, block, width)
     right = picked[:, 1].reshape(number, seg_count, block, width)
     left_all = lax.all_to_all(left, "tm", split_axis=2, concat_axis=1, tiled=True)
-    right_all = lax.all_gather(right, "tm", axis=1, tiled=True)
+    right_all = jnp.concatenate(
+        lax.all_to_all(jnp.stack([right] * lax.axis_size("tm")), "tm", 0, 0), axis=1
+    )
     left_real = left_all[..., :NF]
     left_imag = left_all[..., NF:]
     right_real = right_all[..., :NF]

time: 260 us -> 282 us (1.085)
  waiting for transfers between devices: 175 us -> 196 us
  starting transfers between devices: 12.6 us -> 17.8 us
    all_to_all x0 -> x1, waiting for transfers between devices: none -> 34 us  [shards(): lax.all_to_all(jnp.stack([right] * lax.axis_size('tm')), 'tm', 0, 0)]
    all_gather x1 -> x0, waiting for transfers between devices: 13.7 us -> none  [shards(): right_all = lax.all_gather(right, 'tm', axis=1, tiled=True)]
    unnamed x17 -> x15, local copies, waits for them, and re-layouts: 8.55 us -> 3.01 us
    all_to_all x0 -> x1, starting transfers between devices: none -> 5.19 us  [shards(): lax.all_to_all(jnp.stack([right] * lax.axis_size('tm')), 'tm', 0, 0)]
    reshape x0 -> x1, local copies, waits for them, and re-layouts: none -> 4.17 us  [shards(): jnp.concatenate(lax.all_to_all(jnp.stack([right] * lax.axis_size('tm')),...]
    another operation x1 -> x2, local copies, waits for them, and re-layouts: 0.77 us -> 4.8 us  [shards(): jnp.stack([right] * lax.axis_size('tm'))]
    slice x1 -> x0, local copies, waits for them, and re-layouts: 3.95 us -> none  [shards(): right_imag = right_all[..., NF:]]
  transfers between devices with their start and end apart: 3 -> 3, of which waited for: 3 -> 3; matrix products, arithmetic and copies ran while one was open for 2% -> 1% of each run, Pallas kernels for 0% -> 0%
where the time goes in v1:
time: 282 us
  waiting for transfers between devices  196 us (70%)
  local copies, waits for them, and re-layouts  28.8 us (10%)
  matrix products  22.7 us (8%)
  starting transfers between devices  17.8 us (6%)
  between operations  14.2 us (5%)
    all_gather x1, waiting for transfers between devices, shards(): every = lax.all_gather(white[None], 'pair', axis=0, tiled=True)  154 us
    all_to_all x1, waiting for transfers between devices, shards(): lax.all_to_all(jnp.stack([right] * lax.axis_size('tm')), 'tm', 0, 0)  34 us
    all_to_all x1, starting transfers between devices, shards(): lax.all_to_all(left, 'tm', split_axis=2, concat_axis=1, tiled=True)  12.6 us
    all_to_all x1, waiting for transfers between devices, shards(): lax.all_to_all(left, 'tm', split_axis=2, concat_axis=1, tiled=True)  7.63 us
  transfers between devices with their start and end apart: 3, of which 3 were waited for; matrix products, arithmetic and copies ran while one was open for 1% of the time, Pallas kernels for 0%

profile of v1, /device:TPU:1, one launch (start us, length us, event | category | flops | bytes accessed | tf_op | source)
XLA Modules:
  0.0 282.1 jit_solution(18360366062789378446)
XLA Ops:
  6.6 2.1 fusion.15
  8.6 1.8 convolution_bitcast_fusion
  10.8 0.8 copy.54
  12.0 154.3 %all-gather.2.cloned.1.call-done = bf16[64,256,256]{2,1,0:T(8,128)(2,1)} async-done(((bf16[1,256,256]{2,1,0:T(8,128)(2,1)}), bf16[64,256,256]{2,1,0:T(8,128)(2,1)}) %all-gather.2.cloned.1.call-update) | async-done | bytes 8388624 | tf_op jit(solution)/shard_map/all_gather | solution.py:68
  166.3 4.0 %gather_fusion = bf16[6,256,256]{2,1,0:T(8,128)(2,1)S(1)} fusion(bf16[64,256,256]{2,1,0:T(8,128)(2,1)} %all-gather.2.cloned.1.call-done, s32[1024]{0:T(1024)S(1)} %pad_clamp_fusion), kind=kCustom, calls=%fused_computation | custom fusion | bytes 1572888 | tf_op jit(solution)/shard_map/jit(_take)/gather | solution.py:70
  170.5 1.2 copy.55
  171.6 12.6 %all-to-all-start = ((bf16[3,2,128,256]{3,1,0,2:T(2,128)(2,1)}), bf16[3,2,128,256]{3,1,0,2:T(2,128)(2,1)S(1)}, u32[]{:S(2)}, u32[]{:S(2)}) async-start(bf16[3,2,128,256]{3,1,0,2:T(2,128)(2,1)} %copy.55), calls=%async_computation | async-start | bytes 786432 | tf_op jit(solution)/shard_map/all_to_all | solution.py:74
  184.2 0.4 copy.59
  184.6 7.6 %all-to-all-done = bf16[3,2,128,256]{3,1,0,2:T(2,128)(2,1)S(1)} async-done(((bf16[3,2,128,256]{3,1,0,2:T(2,128)(2,1)}), bf16[3,2,128,256]{3,1,0,2:T(2,128)(2,1)S(1)}, u32[]{:S(2)}, u32[]{:S(2)}) %all-to-all-start) | async-done | bytes 393248 | tf_op jit(solution)/shard_map/all_to_all | solution.py:74
  192.3 4.4 %stack.3 = bf16[8,3,2,128,256]{3,2,4,1,0:T(2,128)(2,1)} broadcast(bf16[3,2,128,256]{2,1,3,0:T(2,128)(2,1)S(1)} %copy.59), dimensions={1,2,3,4} | broadcast | bytes 3538944 | tf_op jit(solution)/shard_map/stack | solution.py:76
  196.6 5.2 %all-to-all-start.1 = ((bf16[8,3,2,128,256]{3,2,4,1,0:T(2,128)(2,1)}), bf16[8,3,2,128,256]{3,2,4,1,0:T(2,128)(2,1)}, u32[]{:S(2)}, u32[]{:S(2)}) async-start(bf16[8,3,2,128,256]{3,2,4,1,0:T(2,128)(2,1)} %stack.3), calls=%async_computation.1 | async-start | bytes 6291456 | tf_op jit(solution)/shard_map/all_to_all | solution.py:76
  202.6 1.8 copy.69
  204.4 1.1 copy.70
  205.5 34.0 %all-to-all-done.1 = bf16[8,3,2,128,256]{3,2,4,1,0:T(2,128)(2,1)} async-done(((bf16[8,3,2,128,256]{3,2,4,1,0:T(2,128)(2,1)}), bf16[8,3,2,128,256]{3,2,4,1,0:T(2,128)(2,1)}, u32[]{:S(2)}, u32[]{:S(2)}) %all-to-all-start.1) | async-done | bytes 3145760 | tf_op jit(solution)/shard_map/all_to_all | solution.py:76
  239.5 4.2 %copy.60 = bf16[3,8,2,128,256]{3,2,1,4,0:T(2,128)(2,1)S(1)} copy(bf16[3,8,2,128,256]{3,2,4,0,1:T(2,128)(2,1)} %bitcast.11) | data formatting | bytes 6291456 | tf_op jit(solution)/shard_map/reshape | solution.py:75
  243.7 0.9 fusion
  244.6 2.6 fusion.4
  247.3 2.7 convolution_subtract_fusion
  249.9 3.5 %copy.68 = f32[3,128,16,128]{1,3,2,0:T(8,128)} copy(f32[3,128,16,128]{3,2,1,0:T(8,128)} %convolution_subtract_fusion) | data formatting | bytes 6291456 | tf_op jit(solution)/shard_map/reshape | solution.py:95
  253.5 5.0 %convolution_add_fusion = f32[3,128,16,128]{3,2,1,0:T(8,128)} fusion(f32[3,128,16,128]{3,2,1,0:T(8,128)} %fusion.4, bf16[3,16,16,128]{1,2,3,0:T(8,128)(2,1)S(1)} %copy.70, bf16[3,16,128,256]{2,1,3,0:T(8,128)(2,1)} %bitcast.41), kind=kOutput, calls=%fused_computation.3 | convolution fusion | flops 25952256 | bytes 8060928 | tf_op jit(solution)/shard_map/qsif,qsjf->qfij/dot_general | solution.py:85
  258.5 3.5 %copy.67 = f32[3,128,16,128]{1,3,2,0:T(8,128)} copy(f32[3,128,16,128]{3,2,1,0:T(8,128)} %convolution_add_fusion) | data formatting | bytes 6291456 | tf_op jit(solution)/shard_map/reshape | solution.py:94
  262.0 5.0 %fusion.22 = f32[3,2048,128]{2,1,0:T(8,128)S(1)} fusion(f32[3,128,2048]{1,2,0:T(8,128)} %bitcast.43, s32[128]{0:T(128)S(1)} %get-tuple-element.16, s32[128]{0:T(128)S(1)} %get-tuple-element.15), kind=kOutput, calls=%fused_computation.43 | convolution fusion | flops 1208188928 | bytes 6292480 | tf_op jit(solution)/shard_map/lf,qfx->qlx/dot_general | solution.py:96
  267.0 4.7 %multiply_bitcast_fusion = f32[3,128,2048]{1,2,0:T(8,128)} fusion(f32[3,2048,128]{2,1,0:T(8,128)S(1)} %fusion.22, f32[3,128,2048]{1,2,0:T(8,128)S(1)} %bitcast.42, f32[3]{0:T(128)S(1)} %compare_select_fusion.3, s32[128]{0:T(128)S(1)} %get-tuple-element.16, s32[128]{0:T(128)S(1)} %get-tuple-element.15), kind=kOutput, calls=%fused_computation.1 | convolution fusion | flops 1209778176 | bytes 9438220 | tf_op jit(solution)/shard_map/lf,qfx->qlx/dot_general | solution.py:97
  271.7 3.5 %copy.64 = f32[3,128,2048]{2,1,0:T(8,128)} copy(f32[3,128,2048]{1,2,0:T(8,128)} %multiply_bitcast_fusion) | data formatting | bytes 6291456 | tf_op jit(solution)/shard_map/mul | solution.py:102
  (34 shorter events, 1.1 us)
Async XLA Ops:
  6.5 2.1 copy-start
  6.5 5.0 %copy-start.4 = (s32[3,2]{0,1:T(2,128)S(1)}, s32[3,2]{0,1:T(2,128)}, u32[]{:S(2)}) copy-start(s32[3,2]{0,1:T(2,128)} %param.6) | copy-start | bytes 76
  6.5 5.1 %copy-start.5 = (s32[64]{0:T(128)S(1)}, s32[64]{0:T(128)}, u32[]{:S(2)}) copy-start(s32[64]{0:T(128)} %param.5) | copy-start | bytes 772
  6.5 159.7 %all-gather.2.cloned.1.call-start = ((), (), s32[]{:S(2)}) async-start(), calls=%async_computation.2 | async-start | bytes 8519680 | tf_op jit(solution)/shard_map/all_gather | solution.py:68
  171.6 20.6 %all-to-all-start = ((bf16[3,2,128,256]{3,1,0,2:T(2,128)(2,1)}), bf16[3,2,128,256]{3,1,0,2:T(2,128)(2,1)S(1)}, u32[]{:S(2)}, u32[]{:S(2)}) async-start(bf16[3,2,128,256]{3,1,0,2:T(2,128)(2,1)} %copy.55), calls=%async_computation | async-start | bytes 786432 | tf_op jit(solution)/shard_map/all_to_all | solution.py:74
  196.6 42.9 %all-to-all-start.1 = ((bf16[8,3,2,128,256]{3,2,4,1,0:T(2,128)(2,1)}), bf16[8,3,2,128,256]{3,2,4,1,0:T(2,128)(2,1)}, u32[]{:S(2)}, u32[]{:S(2)}) async-start(bf16[8,3,2,128,256]{3,2,4,1,0:T(2,128)(2,1)} %stack.3), calls=%async_computation.1 | async-start | bytes 6291456 | tf_op jit(solution)/shard_map/all_to_all | solution.py:76
  239.5 4.2 %copy-start.2 = (bf16[3,16,16,128]{1,2,3,0:T(8,128)(2,1)S(1)}, bf16[3,16,16,128]{1,2,3,0:T(8,128)(2,1)}, u32[]{:S(2)}) copy-start(bf16[3,16,16,128]{1,2,3,0:T(8,128)(2,1)} %copy.69) | copy-start | bytes 589828
  243.7 3.6 %copy-start.1 = (bf16[3,8,2,128,256]{3,2,1,4,0:T(2,128)(2,1)}, bf16[3,8,2,128,256]{3,2,1,4,0:T(2,128)(2,1)S(1)}, u32[]{:S(2)}) copy-start(bf16[3,8,2,128,256]{3,2,1,4,0:T(2,128)(2,1)S(1)} %copy.60) | copy-start | bytes 9437188
  262.0 5.0 %copy-start.3 = (f32[3,128,16,128]{1,3,2,0:T(8,128)S(1)}, f32[3,128,16,128]{1,3,2,0:T(8,128)}, u32[]{:S(2)}) copy-start(f32[3,128,16,128]{1,3,2,0:T(8,128)} %copy.68) | copy-start | bytes 9437188
Sparse Core Ops, SparseCore 0:
  11.7 154.5 all-gather.1
